TPU v7x, 128 devices: a whole 4x4x4 slice. The times are simulated.
128 devices in a mesh: dp: 32 (over x, z, y_hi), mp: 4 (over y_lo, core).
Axes of the slice: x: 4, y: 4 (y_hi: 2, y_lo: 2; y = y_hi * 2 + y_lo), z: 4, core: 2. Of those that a mesh axis runs over, the one named last changes fastest.
Arguments:
- activations: bfloat16 [32768, 8192], P('dp', 'mp'), may hold values from -6 to 6
- cot_true: bfloat16 [32768, 1024], P('dp', 'mp'), may hold values from -6 to 6
- cot_sampled: bfloat16 [32768, 1024], P('dp', 'mp'), may hold values from -6 to 6
- tile_mask: int32 [64, 8], replicated, may hold values from 0 to 1, as said below
- moment: float32 [8192, 1024], P('dp', 'mp'), may hold values from -0.0012207031 to 0.0012207031
- curvature: float32 [8192, 1024], P('dp', 'mp'), may hold values from 0.003 to 3
Outputs:
- update: float32 [8192, 1024], P('dp', 'mp')
- new_curvature: float32 [8192, 1024], P('dp', 'mp')
Inputs may be any that keep to these rules, and one draw needn't show every extreme that they name: Every column of tile_mask holds exactly 16 ones.
All inputs are finite; a program needn't handle non-finite values.
Results may differ from a plain program's by a relative error of at most 0.0003.
Values may be sent and summed in bfloat16 or wider, within the bound.
A program may use at most 128 MiB of HBM per device.

v0:
```python
import jax
import jax.numpy as jnp
from jax import lax
from jax.sharding import PartitionSpec as P

D = 8192
BLOCK = 128
BETA_ONE = 0.965
BETA_TWO = 0.99
GAMMA_CLIP = 0.01
CONTRACT = (((0,), (0,)), ((), ()))


def expand_tiles(tile_grid, tile_width):
    return jnp.repeat(jnp.repeat(tile_grid, tile_width, axis=0), tile_width, axis=1).astype(
        jnp.float32
    )


def on_device(activations, cot_true, cot_sampled, tile_mask, moment, curvature):
    dp_count = lax.axis_size("dp")
    kv_cols = cot_true.shape[1]
    col_tiles = kv_cols // BLOCK
    row_count = D // dp_count
    tokens_all = activations.shape[0] * dp_count
    inv_tokens = 1.0 / tokens_all
    panel = lax.all_gather(activations, "mp", axis=1, tiled=True)
    cotangents = jnp.concatenate([cot_true, cot_sampled], axis=1)
    local_tiles = lax.dynamic_slice_in_dim(
        tile_mask, lax.axis_index("mp") * col_tiles, col_tiles, 1
    )
    owned_tiles = row_count // BLOCK
    first_tile = lax.axis_index("dp") * owned_tiles
    product = lax.dot_general(panel, cotangents, CONTRACT, preferred_element_type=jnp.float32)
    row_mask = expand_tiles(local_tiles, BLOCK)
    owned = lax.psum_scatter(
        product * inv_tokens * jnp.concatenate([row_mask, row_mask], axis=1),
        "dp",
        scatter_dimension=0,
        tiled=True,
    )
    owned_mask = expand_tiles(
        lax.dynamic_slice_in_dim(local_tiles, first_tile, owned_tiles, 0), BLOCK
    )
    grad_true = owned[:, :kv_cols]
    grad_sampled = owned[:, kv_cols:]
    moment_new = BETA_ONE * moment + (1.0 - BETA_ONE) * grad_true
    hessian = tokens_all * grad_sampled * grad_sampled
    curvature_next = BETA_TWO * curvature + (1.0 - BETA_TWO) * hessian
    update = jnp.clip(moment_new / (GAMMA_CLIP * curvature_next), -1.0, 1.0) * owned_mask
    return (update, curvature_next * owned_mask)


def solution(mesh):
    return jax.shard_map(
        on_device,
        mesh=mesh,
        in_specs=(P("dp", "mp"), P("dp", "mp"), P("dp", "mp"), P(), P("dp", "mp"), P("dp", "mp")),
        out_specs=(P("dp", "mp"), P("dp", "mp")),
        check_vma=False,
    )
```

profile of v0, /device:TPU:82, one launch (start us, length us, event | category | flops | bytes accessed | tf_op | source)
XLA Modules:
  0.0 553.9 jit_solution(4977731851931626802)
XLA Ops:
  7.2 0.0 all-gather.2.cloned.1.call-start
  7.2 0.7 all-gather.2.cloned.1.call-update
  7.9 0.0 reduce-scatter.2.cloned.1.call-start
  7.9 0.7 dynamic-slice_convert_fusion.1
  8.6 0.1 broadcast_bitcast_fusion
  8.7 0.1 copy.16
  8.8 151.7 %all-gather.2.cloned.1.call-done = bf16[1024,8192]{1,0:T(8,128)(2,1)} async-done(((bf16[1024,2048]{1,0:T(8,128)(2,1)}), bf16[1024,8192]{1,0:T(8,128)(2,1)}) %all-gather.2.cloned.1.call-update) | async-done | bytes 16777232 | tf_op jit(solution)/shard_map/all_gather | solution.py:27
  160.5 0.9 broadcast_in_dim.13
  161.4 16.2 %maximum_multiply_fusion = f32[8192,512]{0,1:T(8,128)} fusion(f32[8192,256]{0,1:T(8,128)S(1)} %bitcast.21, bf16[1024,8192]{1,0:T(8,128)(2,1)} %all-gather.2.cloned.1.call-done, bf16[1024,256]{1,0:T(8,128)(2,1)} %param.8, bf16[1024,256]{1,0:T(8,128)(2,1)} %param.7), kind=kOutput, calls=%fused_computation | convolution fusion | flops 8604614656 | bytes 42991616 | tf_op jit(solution)/shard_map/dot_general | solution.py:34
  177.6 0.0 copy-start
  177.6 0.0 copy-start.1
  177.6 0.0 reduce-scatter.2.cloned.1.call-update
  177.6 0.8 dynamic-slice_convert_fusion
  178.5 0.1 broadcast_bitcast_fusion.1
  178.5 0.0 copy-done
  178.6 0.1 copy.8
  178.7 0.0 copy-done.1
  178.7 0.1 copy.9
  178.8 365.4 %reduce-scatter.2.cloned.1.call-done = f32[256,512]{0,1:T(8,128)} async-done(((f32[8192,512]{0,1:T(8,128)}), f32[256,512]{0,1:T(8,128)}) %reduce-scatter.2.cloned.1.call-update) | async-done | bytes 524304 | tf_op jit(solution)/shard_map/reduce_scatter | solution.py:36
  544.2 1.2 bitcast_multiply_fusion
  545.4 0.8 copy.10
  546.2 0.8 copy.11
  (1 shorter events, 0.0 us)
Async XLA Ops:
  7.2 153.3 %all-gather.2.cloned.1.call-start = ((), (), s32[]{:S(2)}) async-start(), calls=%async_computation.1 | async-start | bytes 20971520 | tf_op jit(solution)/shard_map/all_gather | solution.py:27
  7.9 536.3 %reduce-scatter.2.cloned.1.call-start = ((), (), s32[]{:S(2)}) async-start(), calls=%async_computation.2 | async-start | bytes 17301504 | tf_op jit(solution)/shard_map/reduce_scatter | solution.py:36
  177.6 0.9 copy-start
  177.6 1.1 copy-start.1
Sparse Core Ops, SparseCore 0:
  9.6 150.8 all-gather.1
  177.8 366.4 reduce-scatter.1
where the time goes:
time: 554 us
  waiting for transfers between devices  518 us (94%)
  matrix products  16.2 us (3%)
  between operations  14.1 us (3%)
    reduce_scatter x1, waiting for transfers between devices, on_device(): lax.psum_scatter(product * inv_tokens * jnp.concatenate([row_mask, row_ma...  365 us
    all_gather x1, waiting for transfers between devices, on_device(): panel = lax.all_gather(activations, 'mp', axis=1, tiled=True)  152 us
    dot_general x1, matrix products, on_device(): lax.dot_general(panel, cotangents, CONTRACT, preferred_element_type=jnp.f...  16.2 us
  transfers between devices with their start and end apart: 2, of which 2 were waited for; matrix products, arithmetic and copies ran while one was open for 0% of the time, Pallas kernels for 0%

commit v1 on v0

--- a/solution.py
+++ b/solution.py
@@ -24,7 +24,8 @@
     row_count = D // dp_count
     tokens_all = activations.shape[0] * dp_count
     inv_tokens = 1.0 / tokens_all
-    panel = lax.all_gather(activations, "mp", axis=1, tiled=True)
+    sent = jnp.stack([activations] * lax.axis_size("mp"))
+    panel = jnp.concatenate(lax.all_to_all(sent, "mp", 0, 0), axis=1)
     cotangents = jnp.concatenate([cot_true, cot_sampled], axis=1)
     local_tiles = lax.dynamic_slice_in_dim(
         tile_mask, lax.axis_index("mp") * col_tiles, col_tiles, 1

time: 554 us -> 612 us (1.10)
  waiting for transfers between devices: 518 us -> 547 us
  local copies, waits for them, and re-layouts: 3.09 us -> 20.9 us
  starting transfers between devices: 0.08 us -> 7.15 us
    all_to_all x0 -> x1, waiting for transfers between devices: none -> 183 us  [on_device(): panel = jnp.concatenate(lax.all_to_all(sent, 'mp', 0, 0), axis=1)]
    all_gather x1 -> x0, waiting for transfers between devices: 152 us -> none  [on_device(): panel = lax.all_gather(activations, 'mp', axis=1, tiled=True)]
    another operation x0 -> x1, local copies, waits for them, and re-layouts: none -> 7.46 us  [on_device(): sent = jnp.stack([activations] * lax.axis_size('mp'))]
    unnamed x12 -> x19, local copies, waits for them, and re-layouts: 2.16 us -> 9.3 us
    all_to_all x0 -> x1, starting transfers between devices: none -> 7.11 us  [on_device(): panel = jnp.concatenate(lax.all_to_all(sent, 'mp', 0, 0), axis=1)]
where the time goes in v1:
time: 612 us
  waiting for transfers between devices  547 us (89%)
  matrix products  21.4 us (3%)
  local copies, waits for them, and re-layouts  20.9 us (3%)
  between operations  14.1 us (2%)
  starting transfers between devices  7.15 us (1%)
    reduce_scatter x1, waiting for transfers between devices, on_device(): lax.psum_scatter(product * inv_tokens * jnp.concatenate([row_mask, row_ma...  364 us
    all_to_all x1, waiting for transfers between devices, on_device(): panel = jnp.concatenate(lax.all_to_all(sent, 'mp', 0, 0), axis=1)  183 us
    dot_general x1, matrix products, on_device(): lax.dot_general(panel, cotangents, CONTRACT, preferred_element_type=jnp.f...  21.4 us
  transfers between devices with their start and end apart: 2, of which 2 were waited for; matrix products, arithmetic and copies ran while one was open for 0% of the time, Pallas kernels for 0%

profile of v1, /device:TPU:82, one launch (start us, length us, event | category | flops | bytes accessed | tf_op | source)
XLA Modules:
  0.0 611.9 jit_solution(14547119893580252377)
XLA Ops:
  7.2 6.4 %copy.13 = bf16[1024,2048]{0,1:T(8,128)(2,1)} copy(bf16[1024,2048]{1,0:T(8,128)(2,1)} %param.6) | data formatting | bytes 8388608 | tf_op args[0]
  13.6 7.5 %stack.2 = bf16[4,1024,2048]{1,2,0:T(8,128)(2,1)} broadcast(bf16[1024,2048]{0,1:T(8,128)(2,1)} %copy.13), dimensions={1,2} | broadcast | bytes 20971520 | tf_op jit(solution)/shard_map/stack | solution.py:27
  21.0 0.0 copy-start.2
  21.0 0.0 copy-start.3
  21.0 0.0 copy-start.4
  21.0 7.1 %all-to-all-start = ((bf16[4,1024,2048]{1,2,0:T(8,128)(2,1)}), bf16[4,1024,2048]{1,2,0:T(8,128)(2,1)}, u32[]{:S(2)}, u32[]{:S(2)}) async-start(bf16[4,1024,2048]{1,2,0:T(8,128)(2,1)} %stack.2), calls=%async_computation | async-start | bytes 33554432 | tf_op jit(solution)/shard_map/all_to_all | solution.py:28
  28.1 0.0 reduce-scatter.2.cloned.1.call-start
  28.2 0.0 copy-done.2
  28.2 0.1 broadcast_bitcast_fusion
  28.3 0.1 copy.21
  28.4 182.8 %all-to-all-done = bf16[4,1024,2048]{1,2,0:T(8,128)(2,1)} async-done(((bf16[4,1024,2048]{1,2,0:T(8,128)(2,1)}), bf16[4,1024,2048]{1,2,0:T(8,128)(2,1)}, u32[]{:S(2)}, u32[]{:S(2)}) %all-to-all-start) | async-done | bytes 16777248 | tf_op jit(solution)/shard_map/all_to_all | solution.py:28
  211.2 4.2 broadcast_in_dim.13
  215.3 0.0 copy-done.3
  215.3 0.0 copy-done.4
  215.3 21.4 %maximum_multiply_fusion = f32[8192,512]{0,1:T(8,128)} fusion(f32[8192,256]{0,1:T(8,128)} %bitcast.24, bf16[1024,8192]{0,1:T(8,128)(2,1)} %bitcast.1, bf16[1024,256]{1,0:T(8,128)(2,1)S(1)} %copy-done.3, bf16[1024,256]{1,0:T(8,128)(2,1)S(1)} %copy-done.4), kind=kOutput, calls=%fused_computation | convolution fusion | flops 8604614656 | bytes 42991616 | tf_op jit(solution)/shard_map/dot_general | solution.py:35
  236.7 0.0 copy-start
  236.7 0.0 copy-start.1
  236.7 0.0 reduce-scatter.2.cloned.1.call-update
  236.8 0.1 dynamic-slice_convert_fusion
  236.8 0.1 broadcast_bitcast_fusion.1
  236.9 0.8 copy-done
  237.7 0.1 copy.12
  237.8 0.0 copy-done.1
  237.8 0.1 copy.14
  237.9 364.3 %reduce-scatter.2.cloned.1.call-done = f32[256,512]{0,1:T(8,128)} async-done(((f32[8192,512]{0,1:T(8,128)}), f32[256,512]{0,1:T(8,128)}) %reduce-scatter.2.cloned.1.call-update) | async-done | bytes 524304 | tf_op jit(solution)/shard_map/reduce_scatter | solution.py:37
  602.2 1.2 bitcast_multiply_fusion
  603.4 0.8 copy.15
  604.2 0.8 copy.16
  (2 shorter events, 0.0 us)
Async XLA Ops:
  21.0 7.2 %copy-start.2 = (s32[64,8]{0,1:T(8,128)S(1)}, s32[64,8]{0,1:T(8,128)}, u32[]{:S(2)}) copy-start(s32[64,8]{0,1:T(8,128)} %param.9) | copy-start | bytes 6148
  21.0 194.3 %copy-start.3 = (bf16[1024,256]{1,0:T(8,128)(2,1)S(1)}, bf16[1024,256]{1,0:T(8,128)(2,1)}, u32[]{:S(2)}) copy-start(bf16[1024,256]{1,0:T(8,128)(2,1)} %param.8) | copy-start | bytes 1572868
  21.0 194.3 %copy-start.4 = (bf16[1024,256]{1,0:T(8,128)(2,1)S(1)}, bf16[1024,256]{1,0:T(8,128)(2,1)}, u32[]{:S(2)}) copy-start(bf16[1024,256]{1,0:T(8,128)(2,1)} %param.7) | copy-start | bytes 1572868
  21.0 190.1 %all-to-all-start = ((bf16[4,1024,2048]{1,2,0:T(8,128)(2,1)}), bf16[4,1024,2048]{1,2,0:T(8,128)(2,1)}, u32[]{:S(2)}, u32[]{:S(2)}) async-start(bf16[4,1024,2048]{1,2,0:T(8,128)(2,1)} %stack.2), calls=%async_computation | async-start | bytes 33554432 | tf_op jit(solution)/shard_map/all_to_all | solution.py:28
  28.1 574.1 %reduce-scatter.2.cloned.1.call-start = ((), (), s32[]{:S(2)}) async-start(), calls=%async_computation.2 | async-start | bytes 17301504 | tf_op jit(solution)/shard_map/reduce_scatter | solution.py:37
  236.7 0.9 copy-start
  236.7 1.1 copy-start.1
Sparse Core Ops, SparseCore 0:
  236.9 365.2 reduce-scatter.1
